TPU v7x, 32 devices: a whole 2x2x4 slice. The times are simulated.
32 devices in a mesh: rep: 2 (over x), idx: 16 (over z, y, core).
Axes of the slice: x: 2, y: 2, z: 4, core: 2. Of those that a mesh axis runs over, the one named last changes fastest.
Arguments:
- images: bfloat16 [16448, 1408], P(('rep', 'idx')), parts along dimension 0, may hold values from -6 to 6
- norm_gain: float32 [1408], replicated, may hold values from 0.25 to 1.75
- qkv_values: bfloat16 [1408, 4224], P(None, 'idx'), may hold values from -0.5 to 0.5
- qkv_exponents: int32 [11, 4224], replicated, may hold values from -2 to 2
- proj_values: bfloat16 [1408, 1408], P(None, 'idx'), may hold values from -0.078125 to 0.078125
- proj_exponents: int32 [11, 1408], replicated, may hold values from -2 to 2
- captions: bfloat16 [32768, 1408], P(('rep', 'idx')), parts along dimension 0, may hold values from -0.15625 to 0.15625
- owners: int32 [16448, 1], P(('rep', 'idx')), parts along dimension 0, may hold values from 0 to 15; in each aligned block of 514 rows (0 to 513, 514 to 1027, ...) at most 34 rows name the same one
- candidates: int32 [16448, 4], P(('rep', 'idx')), parts along dimension 0, may hold values from 0 to 7, all different within a row
Outputs:
- embedding: bfloat16 [16448, 1408], P(('rep', 'idx')), parts along dimension 0
- scores: bfloat16 [16448, 4, 128], P(('rep', 'idx')), parts along dimension 0
There are 2 independent parts, one for each index of `rep`. A program takes and returns all parts, laid end to end along the dimension named above; an argument that names none is the same for every part. Nothing has to cross between parts.
Inputs may be any that keep to these rules, and one draw needn't show every extreme that they name: `owners`: among the tokens of one device no owner is named more than 34 times, a bound that some block reaches. `candidates`: each token names 4 different caption blocks.
All inputs are finite; a program needn't handle non-finite values.
Results may differ from a plain program's by a relative error of at most 0.004.
The roundings to bfloat16 on the way count: a program that leaves them out, or rounds other values in their place, can miss the bound.
Values may be sent and summed in bfloat16 or wider, within the bound.
A program may use at most 192 MiB of HBM per device.

v0:
```python
import jax
import jax.numpy as jnp
from jax import lax
from jax.sharding import PartitionSpec as P

HEADS = 16
PATCHES = 257
CBLK = 8
CAPT = 128


def dequant(stored, exponents):
    row_count, col_count = stored.shape
    block_count = exponents.shape[0]
    scaled = stored.astype(jnp.float32).reshape(block_count, row_count // block_count, col_count)
    scaled = scaled * jnp.exp2(exponents.astype(jnp.float32))[:, None, :]
    return scaled.reshape(row_count, col_count).astype(jnp.bfloat16)


def layer_norm(token_rows, norm_gain):
    values = token_rows.astype(jnp.float32)
    centered = values - jnp.mean(values, axis=-1, keepdims=True)
    inv_scale = lax.rsqrt(jnp.mean(centered * centered, axis=-1, keepdims=True) + 1e-06)
    return (centered * inv_scale * norm_gain).astype(jnp.bfloat16)


def attend(qkv_rows, model_width):
    head_dim = model_width // HEADS
    grouped = qkv_rows.reshape(-1, PATCHES, 3, HEADS, head_dim)
    logits = jnp.einsum(
        "gqhd,gkhd->ghqk", grouped[:, :, 0], grouped[:, :, 1], preferred_element_type=jnp.float32
    )
    logits = logits * head_dim ** (-0.5)
    logits = logits - jnp.max(logits, axis=-1, keepdims=True)
    weights = jnp.exp(logits)
    attn_probs = (weights / jnp.sum(weights, axis=-1, keepdims=True)).astype(jnp.bfloat16)
    mixed_heads = jnp.einsum(
        "ghqk,gkhd->gqhd", attn_probs, grouped[:, :, 2], preferred_element_type=jnp.float32
    )
    return mixed_heads.astype(jnp.bfloat16).reshape(-1, model_width)


def project_with(left_rows, exponents, col_piece):
    return jnp.dot(left_rows, dequant(col_piece, exponents), preferred_element_type=jnp.float32)


def score_with(captions):

    def score_slots(slot_parts):
        slot_rows, slot_picks = slot_parts
        peer_count, item_count = (slot_rows.shape[0], slot_rows.shape[1])
        flat_rows = slot_rows.reshape(peer_count * item_count, slot_rows.shape[2])
        all_scores = lax.dot_general(
            flat_rows, captions, (((1,), (1,)), ((), ())), preferred_element_type=jnp.float32
        )
        all_scores = all_scores.reshape(peer_count * item_count, CBLK, CAPT)
        block_index = jnp.clip(
            slot_picks.reshape(peer_count * item_count, -1).astype(jnp.int32), 0, CBLK - 1
        )
        chosen = jnp.take_along_axis(all_scores, block_index[:, :, None], axis=1)
        return chosen.astype(jnp.bfloat16).reshape(peer_count, item_count, -1, CAPT)

    return score_slots


def local(
    images,
    norm_gain,
    qkv_values,
    qkv_exponents,
    proj_values,
    proj_exponents,
    captions,
    owners,
    candidates,
):
    model_width = images.shape[1]
    normed = layer_norm(images, norm_gain)
    qkv_rows = project_with(
        normed, qkv_exponents, lax.all_gather(qkv_values, "idx", axis=1, tiled=True)
    ).astype(jnp.bfloat16)
    mixed_heads = attend(qkv_rows, model_width)
    branch = project_with(
        mixed_heads, proj_exponents, lax.all_gather(proj_values, "idx", axis=1, tiled=True)
    )
    hidden = images.astype(jnp.float32) + branch
    inv_scale = lax.rsqrt(jnp.mean(hidden * hidden, axis=-1, keepdims=True) + 1e-06)
    embedding = (hidden * inv_scale).astype(jnp.bfloat16)
    token_count = embedding.shape[0]
    peer_count = lax.axis_size("idx")
    capacity = (token_count + peer_count - 1) // peer_count + 1
    owner_ids = owners[:, 0]
    onehot = (owner_ids[:, None] == jnp.arange(peer_count, dtype=jnp.int32)[None, :]).astype(
        jnp.int32
    )
    slot_rank = jnp.sum((jnp.cumsum(onehot, axis=0) - onehot) * onehot, axis=1)
    slot_index = owner_ids * capacity + slot_rank
    send_rows = (
        jnp.zeros((peer_count * capacity, model_width), jnp.bfloat16).at[slot_index].set(embedding)
    )
    send_rows = send_rows.reshape(peer_count, capacity, model_width)
    pick_count = candidates.shape[1]
    send_picks = (
        jnp.full((peer_count * capacity, pick_count), -1.0, jnp.bfloat16)
        .at[slot_index]
        .set(candidates.astype(jnp.bfloat16))
    )
    send_picks = send_picks.reshape(peer_count, capacity, pick_count)
    score_slots = score_with(captions)
    arrived = (
        lax.all_to_all(send_rows, "idx", split_axis=0, concat_axis=0, tiled=True),
        lax.all_to_all(send_picks, "idx", split_axis=0, concat_axis=0, tiled=True),
    )
    returned = lax.all_to_all(score_slots(arrived), "idx", split_axis=0, concat_axis=0, tiled=True)
    scores = returned.reshape(peer_count * capacity, pick_count, CAPT)[slot_index]
    return (embedding, scores)


def solution(mesh):
    placed = (
        P(("rep", "idx"), None),
        P(),
        P(None, "idx"),
        P(),
        P(None, "idx"),
        P(),
        P(("rep", "idx"), None),
        P(("rep", "idx"), None),
        P(("rep", "idx"), None),
    )
    return jax.shard_map(
        local,
        mesh=mesh,
        in_specs=placed,
        out_specs=(P(("rep", "idx"), None), P(("rep", "idx"), None, None)),
        check_vma=False,
    )
```

profile of v0, /device:TPU:0, one launch (start us, length us, event | category | flops | bytes accessed | tf_op | source)
XLA Modules:
  0.0 386.6 jit_solution(72550061638257239)
XLA Ops:
  7.2 0.0 copy-start
  7.2 0.0 copy-start.2
  7.2 0.0 all-gather.5.cloned.1.call-start
  7.2 0.7 all-gather.5.cloned.1.call-update
  7.9 0.0 all-gather.3.cloned.1.call-start
  8.0 0.7 all-gather.3.cloned.1.call-update
  8.7 0.7 reduce
  9.4 1.4 reduce-window.6
  10.8 0.2 slice_reduce_fusion
  11.1 0.7 convert_element_type.79
  11.8 0.2 copy.41
  12.0 0.1 bitcast_bitcast_fusion
  12.1 0.7 fusion.30
  12.8 4.2 %scatter_custom_fusion = bf16[544,4]{1,0:T(8,128)(2,1)S(1)} fusion(s32[514]{0:T(1024)S(1)} %fusion.30, bf16[514,4]{1,0:T(8,128)(2,1)S(1)} %copy.41, bf16[]{:T(256)} %constant.14.clone.1), kind=kCustom, calls=%fused_computation.40 | custom fusion | bytes 4354 | tf_op jit(solution)/shard_map/scatter | solution.py:106
  17.1 0.0 copy-start.3
  17.1 0.1 copy.42
  17.2 0.1 reshape.110
  17.3 0.6 copy.43
  17.9 7.4 %all-to-all-start = ((bf16[16,34,4]{1,2,0:T(4,128)(2,1)}), bf16[16,34,4]{1,2,0:T(4,128)(2,1)S(1)}, u32[]{:S(2)}, u32[]{:S(2)}) async-start(bf16[16,34,4]{1,2,0:T(4,128)(2,1)} %copy.43), calls=%async_computation | async-start | bytes 32768 | tf_op jit(solution)/shard_map/all_to_all | solution.py:112
  25.4 1.7 convert_reduce_fusion
  27.0 1.9 fusion.10
  29.0 0.0 copy-done.3
  29.0 0.0 copy-done.2
  29.1 33.5 %all-gather.5.cloned.1.call-done = bf16[1408,1408]{0,1:T(8,128)(2,1)} async-done(((bf16[1408,88]{0,1:T(8,128)(2,1)}), bf16[1408,1408]{0,1:T(8,128)(2,1)}) %all-gather.5.cloned.1.call-update) | async-done | bytes 3964944 | tf_op jit(solution)/shard_map/all_gather | solution.py:84
  62.6 6.2 %copy.38 = bf16[1408,1408]{1,0:T(8,128)(2,1)} copy(bf16[1408,1408]{0,1:T(8,128)(2,1)} %all-gather.5.cloned.1.call-done) | data formatting | bytes 7929856 | tf_op jit(solution)/shard_map/all_gather | solution.py:84
  68.8 5.0 %fusion.5 = bf16[1408,1408]{1,0:T(8,128)(2,1)} fusion(bf16[1408,1408]{1,0:T(8,128)(2,1)} %copy.38, f32[11,1408]{1,0:T(8,128)S(1)} %multiply_exponential_fusion.1), kind=kLoop, calls=%fused_computation.12 | loop fusion | flops 5947392 | bytes 7991808 | tf_op jit(solution)/shard_map/convert_element_type | solution.py:17
  73.8 85.8 %all-gather.3.cloned.1.call-done = bf16[1408,4224]{0,1:T(8,128)(2,1)} async-done(((bf16[1408,264]{0,1:T(8,128)(2,1)}), bf16[1408,4224]{0,1:T(8,128)(2,1)}) %all-gather.3.cloned.1.call-update) | async-done | bytes 11894800 | tf_op jit(solution)/shard_map/all_gather | solution.py:80
  159.6 16.0 %copy.32 = bf16[1408,4224]{1,0:T(8,128)(2,1)} copy(bf16[1408,4224]{0,1:T(8,128)(2,1)} %all-gather.3.cloned.1.call-done) | data formatting | bytes 23789568 | tf_op jit(solution)/shard_map/all_gather | solution.py:80
  175.5 0.0 copy-start.1
  175.6 0.0 copy-start.4
  175.6 6.8 %fusion.1 = bf16[1408,4224]{1,0:T(8,128)(2,1)S(1)} fusion(bf16[1408,4224]{1,0:T(8,128)(2,1)} %copy.32, f32[11,4224]{1,0:T(8,128)S(1)} %multiply_exponential_fusion), kind=kLoop, calls=%fused_computation.6 | loop fusion | flops 17842176 | bytes 23975424 | tf_op jit(solution)/shard_map/convert_element_type | solution.py:17
  182.4 0.0 copy-done.1
  182.4 0.0 copy-done.4
  182.4 9.2 %convolution_convert_fusion = bf16[514,4224]{1,0:T(8,128)(2,1)} fusion(bf16[1408,4224]{1,0:T(8,128)(2,1)S(1)} %fusion.1, bf16[514,1408]{1,0:T(8,128)(2,1)S(1)} %copy-done.1, f32[1408]{0:T(1024)S(1)} %copy-done.4, f32[514]{0:T(1024)S(1)} %add_rsqrt_fusion.1, f32[514]{0:T(1024)S(1)} %broadcast_multiply_fusion), kind=kOutput, calls=%fused_computation.13 | convolution fusion | flops 6119708672 | bytes 17694224 | tf_op jit(solution)/shard_map/dot_general | solution.py:44
  191.6 14.7 %reshape.106 = bf16[2,257,3,16,88]{4,3,2,1,0:T(8,128)(2,1)} reshape(bf16[514,4224]{1,0:T(8,128)(2,1)} %convolution_convert_fusion) | data formatting | bytes 8684544 | tf_op jit(solution)/shard_map/reshape | solution.py:29
  206.2 5.3 %fusion.32 = (bf16[2,257,1,16,88]{4,3,2,1,0:T(8,128)(2,1)}, bf16[2,257,1,16,88]{4,3,2,1,0:T(8,128)(2,1)S(1)}, bf16[2,257,1,16,88]{4,3,2,1,0:T(8,128)(2,1)S(1)}) fusion(bf16[2,257,3,16,88]{4,3,2,1,0:T(8,128)(2,1)} %reshape.106), kind=kLoop, calls=%fused_computation.65 | loop fusion | bytes 8684544 | tf_op jit(solution)/shard_map/slice | solution.py:38
  211.5 7.2 %fusion.13 = f32[2,16,257,257]{2,3,1,0:T(8,128)} fusion(bf16[2,257,1,16,88]{4,3,2,1,0:T(8,128)(2,1)S(1)} %get-tuple-element.3, bf16[2,257,1,16,88]{4,3,2,1,0:T(8,128)(2,1)S(1)} %get-tuple-element.4), kind=kOutput, calls=%fused_computation.27 | convolution fusion | flops 371987968 | bytes 11349120 | tf_op jit(solution)/shard_map/gqhd,gkhd->ghqk/dot_general | solution.py:30
  218.7 16.6 %fusion.33 = (f32[2,16,257]{2,1,0:T(8,128)S(1)}, f32[2,16,257,257]{2,3,1,0:T(8,128)}) fusion(f32[2,16,257,257]{2,3,1,0:T(8,128)} %fusion.13), kind=kOutput, calls=%fused_computation.66 | output fusion | flops 8454528 | bytes 16941440 | tf_op jit(solution)/shard_map/sub | solution.py:34
  235.3 4.4 %copy.49 = bf16[2,257,1,16,88]{1,4,3,0,2:T(8,128)(2,1)} copy(bf16[2,257,1,16,88]{4,3,2,1,0:T(8,128)(2,1)} %get-tuple-element.2) | data formatting | bytes 2894848
  239.8 8.5 %convert_bitcast_fusion = bf16[2,257,16,88]{1,3,2,0:T(8,128)(2,1)} fusion(f32[2,16,257,257]{2,3,1,0:T(8,128)} %get-tuple-element.6, f32[2,16,257]{2,1,0:T(8,128)S(1)} %get-tuple-element.5, bf16[2,257,1,16,88]{1,4,3,0,2:T(8,128)(2,1)} %copy.49), kind=kOutput, calls=%fused_computation.30 | convolution fusion | flops 376938816 | bytes 11382016 | tf_op jit(solution)/shard_map/ghqk,gkhd->gqhd/dot_general | solution.py:37
  248.3 4.5 %copy.37 = bf16[2,257,16,88]{3,2,1,0:T(8,128)(2,1)} copy(bf16[2,257,16,88]{1,3,2,0:T(8,128)(2,1)} %convert_bitcast_fusion) | data formatting | bytes 2894848 | tf_op jit(solution)/shard_map/convert_element_type | solution.py:40
  252.8 4.6 %reshape.107 = bf16[514,1408]{1,0:T(8,128)(2,1)} reshape(bf16[2,257,16,88]{3,2,1,0:T(8,128)(2,1)} %copy.37) | data formatting | bytes 2894848 | tf_op jit(solution)/shard_map/reshape | solution.py:40
  257.5 7.3 %multiply_reduce_fusion.1 = (f32[514]{0:T(1024)S(1)}, f32[514,1408]{1,0:T(8,128)}) fusion(bf16[514,1408]{1,0:T(8,128)(2,1)} %reshape.107, bf16[1408,1408]{1,0:T(8,128)(2,1)} %fusion.5, bf16[514,1408]{1,0:T(8,128)(2,1)} %param.9), kind=kOutput, calls=%fused_computation.25 | convolution fusion | flops 2040867328 | bytes 9756680 | tf_op jit(solution)/shard_map/dot_general | solution.py:44
  264.7 12.3 %scatter_custom_fusion.1 = bf16[544,1408]{1,0:T(8,128)(2,1)} fusion(s32[514]{0:T(1024)S(1)} %fusion.30, bf16[]{:T(256)} %constant.45.clone.1, f32[514,1408]{1,0:T(8,128)} %get-tuple-element.8, f32[514]{0:T(1024)S(1)} %add_rsqrt_fusion), kind=kCustom, calls=%fused_computation.35 | custom fusion | flops 1447424 | bytes 4430850 | tf_op jit(solution)/shard_map/scatter | solution.py:99
  277.0 2.6 reshape.111
  279.6 0.0 all-to-all-done
  279.6 4.4 %all-to-all-start.1 = ((bf16[16,34,1408]{2,1,0:T(8,128)(2,1)}), bf16[16,34,1408]{2,1,0:T(8,128)(2,1)}, u32[]{:S(2)}, u32[]{:S(2)}) async-start(bf16[16,34,1408]{2,1,0:T(8,128)(2,1)} %reshape.111), calls=%async_computation.1 | async-start | bytes 3604480 | tf_op jit(solution)/shard_map/all_to_all | solution.py:111
  284.1 0.1 min.12
  284.2 0.1 copy.46
  284.4 0.2 reshape.123
  284.6 0.3 copy.44
  284.9 35.0 %all-to-all-done.1 = bf16[16,34,1408]{2,1,0:T(8,128)(2,1)} async-done(((bf16[16,34,1408]{2,1,0:T(8,128)(2,1)}), bf16[16,34,1408]{2,1,0:T(8,128)(2,1)}, u32[]{:S(2)}, u32[]{:S(2)}) %all-to-all-start.1) | async-done | bytes 1531936 | tf_op jit(solution)/shard_map/all_to_all | solution.py:111
  319.9 2.6 reshape.146
  322.5 0.0 copy-done
  322.5 3.3 fusion.34
  325.8 1.4 copy.47
  327.2 22.9 %gather_fusion.1 = bf16[2176,128]{1,0:T(8,128)(2,1)S(1)} fusion(bf16[544,8,128]{2,1,0:T(8,128)(2,1)} %copy.47, s32[2176]{0:T(1024)S(1)} %reshape.123), kind=kCustom, calls=%fused_computation.1 | custom fusion | bytes 1131520 | tf_op jit(solution)/shard_map/jit(take_along_axis)/gather | solution.py:60
  350.2 1.5 select_convert_fusion
  351.6 10.2 %all-to-all-start.2 = ((bf16[16,34,4,128]{3,2,1,0:T(4,128)(2,1)}), bf16[16,34,4,128]{3,2,1,0:T(4,128)(2,1)S(1)}, u32[]{:S(2)}, u32[]{:S(2)}) async-start(bf16[16,34,4,128]{3,2,1,0:T(4,128)(2,1)} %select_convert_fusion), calls=%async_computation.2 | async-start | bytes 1114112 | tf_op jit(solution)/shard_map/all_to_all | solution.py:114
  361.9 3.2 multiply_convert_fusion
  365.0 11.6 %all-to-all-done.2 = bf16[16,34,4,128]{3,2,1,0:T(4,128)(2,1)S(1)} async-done(((bf16[16,34,4,128]{3,2,1,0:T(4,128)(2,1)}), bf16[16,34,4,128]{3,2,1,0:T(4,128)(2,1)S(1)}, u32[]{:S(2)}, u32[]{:S(2)}) %all-to-all-start.2) | async-done | bytes 557088 | tf_op jit(solution)/shard_map/all_to_all | solution.py:114
  376.7 3.1 gather_fusion
  (14 shorter events, 0.2 us)
Async XLA Ops:
  7.2 315.3 %copy-start = (bf16[1024,1408]{1,0:T(8,128)(2,1)S(1)}, bf16[1024,1408]{1,0:T(8,128)(2,1)}, u32[]{:S(2)}) copy-start(bf16[1024,1408]{1,0:T(8,128)(2,1)} %param.15) | copy-start | bytes 8650756
  7.2 21.8 %copy-start.2 = (s32[11,4224]{1,0:T(8,128)S(1)}, s32[11,4224]{1,0:T(8,128)}, u32[]{:S(2)}) copy-start(s32[11,4224]{1,0:T(8,128)} %param.12) | copy-start | bytes 557572
  7.2 55.4 %all-gather.5.cloned.1.call-start = ((), (), s32[]{:S(2)}) async-start(), calls=%async_computation.4 | async-start | bytes 4212736 | tf_op jit(solution)/shard_map/all_gather | solution.py:84
  7.9 151.7 %all-gather.3.cloned.1.call-start = ((), (), s32[]{:S(2)}) async-start(), calls=%async_computation.3 | async-start | bytes 12638208 | tf_op jit(solution)/shard_map/all_gather | solution.py:80
  17.1 11.9 %copy-start.3 = (s32[11,1408]{1,0:T(8,128)S(1)}, s32[11,1408]{1,0:T(8,128)}, u32[]{:S(2)}) copy-start(s32[11,1408]{1,0:T(8,128)} %param.14) | copy-start | bytes 185860
  17.9 261.7 %all-to-all-start = ((bf16[16,34,4]{1,2,0:T(4,128)(2,1)}), bf16[16,34,4]{1,2,0:T(4,128)(2,1)S(1)}, u32[]{:S(2)}, u32[]{:S(2)}) async-start(bf16[16,34,4]{1,2,0:T(4,128)(2,1)} %copy.43), calls=%async_computation | async-start | bytes 32768 | tf_op jit(solution)/shard_map/all_to_all | solution.py:112
  175.5 6.8 %copy-start.1 = (bf16[514,1408]{1,0:T(8,128)(2,1)S(1)}, bf16[514,1408]{1,0:T(8,128)(2,1)}, u32[]{:S(2)}) copy-start(bf16[514,1408]{1,0:T(8,128)(2,1)} %param.9) | copy-start | bytes 4342276
  175.6 6.8 %copy-start.4 = (f32[1408]{0:T(1024)S(1)}, f32[1408]{0:T(1024)}, u32[]{:S(2)}) copy-start(f32[1408]{0:T(1024)} %param.10) | copy-start | bytes 16900
  279.6 40.3 %all-to-all-start.1 = ((bf16[16,34,1408]{2,1,0:T(8,128)(2,1)}), bf16[16,34,1408]{2,1,0:T(8,128)(2,1)}, u32[]{:S(2)}, u32[]{:S(2)}) async-start(bf16[16,34,1408]{2,1,0:T(8,128)(2,1)} %reshape.111), calls=%async_computation.1 | async-start | bytes 3604480 | tf_op jit(solution)/shard_map/all_to_all | solution.py:111
  351.6 25.0 %all-to-all-start.2 = ((bf16[16,34,4,128]{3,2,1,0:T(4,128)(2,1)}), bf16[16,34,4,128]{3,2,1,0:T(4,128)(2,1)S(1)}, u32[]{:S(2)}, u32[]{:S(2)}) async-start(bf16[16,34,4,128]{3,2,1,0:T(4,128)(2,1)} %select_convert_fusion), calls=%async_computation.2 | async-start | bytes 1114112 | tf_op jit(solution)/shard_map/all_to_all | solution.py:114
Sparse Core Ops, SparseCore 0:
  10.2 52.3 all-gather.4
  64.7 94.8 all-gather.2
where the time goes:
time: 388 us; the launch traced here: 387 us
  waiting for transfers between devices  167 us (43%)
  local copies, waits for them, and re-layouts  94.7 us (24%)
  other arithmetic  52.8 us (14%)
  matrix products  35.4 us (9%)
  starting transfers between devices  22.1 us (6%)
  between operations  14.3 us (4%)
    all_gather x1, waiting for transfers between devices, local(): lax.all_gather(qkv_values, 'idx', axis=1, tiled=True)  85.8 us
    all_to_all x1, waiting for transfers between devices, local(): lax.all_to_all(send_rows, 'idx', split_axis=0, concat_axis=0, tiled=True)  35 us
    all_gather x1, waiting for transfers between devices, local(): lax.all_gather(proj_values, 'idx', axis=1, tiled=True)  33.5 us
    gather x3, local copies, waits for them, and re-layouts, score_slots(): chosen = jnp.take_along_axis(all_scores, block_index[:, :, None], axis=1)  23.3 us
    sub x1, other arithmetic, attend(): logits = logits - jnp.max(logits, axis=-1, keepdims=True)  16.6 us
    dot_general x2, matrix products, project_with(): jnp.dot(left_rows, dequant(col_piece, exponents), preferred_element_type=...  16.4 us
    all_gather x1, local copies, waits for them, and re-layouts, local(): lax.all_gather(qkv_values, 'idx', axis=1, tiled=True)  16 us
    reshape x1, local copies, waits for them, and re-layouts, attend(): grouped = qkv_rows.reshape(-1, PATCHES, 3, HEADS, head_dim)  14.7 us
  transfers between devices with their start and end apart: 5, of which 4 were waited for; matrix products, arithmetic and copies ran while one was open for 38% of the time, Pallas kernels for 0%

commit v1 on v0

--- a/solution.py
+++ b/solution.py
@@ -7,6 +7,29 @@
 PATCHES = 257
 CBLK = 8
 CAPT = 128
+
+
+def cut_along(x, dim, length):
+    shape = x.shape
+    blocks = x.reshape(*shape[:dim], length, shape[dim] // length, *shape[dim + 1 :])
+    return jnp.moveaxis(blocks, dim, 0)
+
+
+def joined_along(blocks, dim):
+    lengths = list(blocks.shape[1:])
+    lengths[dim] *= blocks.shape[0]
+    return jnp.moveaxis(blocks, 0, dim).reshape(lengths)
+
+
+def exchange_directly(x, axis, split_dim, concat_dim):
+    size, index = (lax.axis_size(axis), lax.axis_index(axis))
+    pieces = cut_along(x, split_dim, size)
+    done = [pieces[index]]
+    for step in range(1, size):
+        sent = pieces[(index + step) % size]
+        done.append(lax.ppermute(sent, axis, [(i, (i + step) % size) for i in range(size)]))
+    pieces = jnp.stack(done)[(index - jnp.arange(size)) % size]
+    return joined_along(pieces, concat_dim)
 
 
 def dequant(stored, exponents):
@@ -111,7 +134,7 @@
         lax.all_to_all(send_rows, "idx", split_axis=0, concat_axis=0, tiled=True),
         lax.all_to_all(send_picks, "idx", split_axis=0, concat_axis=0, tiled=True),
     )
-    returned = lax.all_to_all(score_slots(arrived), "idx", split_axis=0, concat_axis=0, tiled=True)
+    returned = exchange_directly(score_slots(arrived), "idx", 0, 0)
     scores = returned.reshape(peer_count * capacity, pick_count, CAPT)[slot_index]
     return (embedding, scores)
 

time: 388 us -> 407 us (1.049); the launches traced: 387 us -> 399 us
  starting transfers between devices: 22.1 us -> 40.8 us
  waiting for transfers between devices: 167 us -> 157 us
  local copies, waits for them, and re-layouts: 94.7 us -> 98.8 us
    ppermute x0 -> x15, starting transfers between devices: none -> 28.7 us  [exchange_directly(): lax.ppermute(sent, axis, [(i, (i + step) % size) for i in range(size)])]
    all_to_all x1 -> x0, waiting for transfers between devices: 11.6 us -> none  [local(): lax.all_to_all(score_slots(arrived), 'idx', split_axis=0, concat_axis=0,...]
    all_to_all x1 -> x0, starting transfers between devices: 10.2 us -> none  [local(): lax.all_to_all(score_slots(arrived), 'idx', split_axis=0, concat_axis=0,...]
  transfers between devices with their start and end apart: 5 -> 19, of which waited for: 4 -> 4; matrix products, arithmetic and copies ran while one was open for 38% -> 37% of each run, Pallas kernels for 0% -> 0%
where the time goes in v1:
time: 407 us; the launch traced here: 399 us
  waiting for transfers between devices  157 us (39%)
  local copies, waits for them, and re-layouts  98.8 us (24%)
  other arithmetic  52.1 us (13%)
  starting transfers between devices  40.8 us (10%)
  matrix products  35.4 us (9%)
  between operations  14.9 us (4%)
    all_gather x1, waiting for transfers between devices, local(): lax.all_gather(qkv_values, 'idx', axis=1, tiled=True)  85.8 us
    all_to_all x1, waiting for transfers between devices, local(): lax.all_to_all(send_rows, 'idx', split_axis=0, concat_axis=0, tiled=True)  34.7 us
    all_gather x1, waiting for transfers between devices, local(): lax.all_gather(proj_values, 'idx', axis=1, tiled=True)  33.5 us
    ppermute x15, starting transfers between devices, exchange_directly(): lax.ppermute(sent, axis, [(i, (i + step) % size) for i in range(size)])  28.7 us
    gather x3, local copies, waits for them, and re-layouts, score_slots(): chosen = jnp.take_along_axis(all_scores, block_index[:, :, None], axis=1)  23.3 us
    sub x1, other arithmetic, attend(): logits = logits - jnp.max(logits, axis=-1, keepdims=True)  16.6 us
    dot_general x2, matrix products, project_with(): jnp.dot(left_rows, dequant(col_piece, exponents), preferred_element_type=...  16.4 us
    all_gather x1, local copies, waits for them, and re-layouts, local(): lax.all_gather(qkv_values, 'idx', axis=1, tiled=True)  16 us
  transfers between devices with their start and end apart: 19, of which 4 were waited for; matrix products, arithmetic and copies ran while one was open for 37% of the time, Pallas kernels for 0%

profile of v1, /device:TPU:0, one launch (start us, length us, event | category | flops | bytes accessed | tf_op | source)
XLA Modules:
  0.0 398.9 jit_solution(11818093786819774328)
XLA Ops:
  7.2 0.7 all-gather.5.cloned.1.call-update
  8.0 0.7 all-gather.3.cloned.1.call-update
  8.7 0.7 reduce
  9.4 1.4 reduce-window.6
  10.8 0.2 slice_reduce_fusion
  11.1 0.7 convert_element_type.85
  11.8 0.2 copy.41
  12.1 0.7 fusion.30
  12.8 4.2 %scatter_custom_fusion = bf16[544,4]{1,0:T(8,128)(2,1)S(1)} fusion(s32[514]{0:T(1024)S(1)} %fusion.30, bf16[514,4]{1,0:T(8,128)(2,1)S(1)} %copy.41, bf16[]{:T(256)} %constant.132.clone.1), kind=kCustom, calls=%fused_computation.41 | custom fusion | bytes 4354 | tf_op jit(solution)/shard_map/scatter | solution.py:129
  17.1 0.1 copy.42
  17.2 0.1 reshape.169
  17.3 0.6 copy.43
  17.9 7.4 %all-to-all-start = ((bf16[16,34,4]{1,2,0:T(4,128)(2,1)}), bf16[16,34,4]{1,2,0:T(4,128)(2,1)S(1)}, u32[]{:S(2)}, u32[]{:S(2)}) async-start(bf16[16,34,4]{1,2,0:T(4,128)(2,1)} %copy.43), calls=%async_computation | async-start | bytes 32768 | tf_op jit(solution)/shard_map/all_to_all | solution.py:135
  25.4 1.7 convert_reduce_fusion
  27.0 1.9 fusion.10
  29.1 33.5 %all-gather.5.cloned.1.call-done = bf16[1408,1408]{0,1:T(8,128)(2,1)} async-done(((bf16[1408,88]{0,1:T(8,128)(2,1)}), bf16[1408,1408]{0,1:T(8,128)(2,1)}) %all-gather.5.cloned.1.call-update) | async-done | bytes 3964944 | tf_op jit(solution)/shard_map/all_gather | solution.py:107
  62.6 6.2 %copy.38 = bf16[1408,1408]{1,0:T(8,128)(2,1)} copy(bf16[1408,1408]{0,1:T(8,128)(2,1)} %all-gather.5.cloned.1.call-done) | data formatting | bytes 7929856 | tf_op jit(solution)/shard_map/all_gather | solution.py:107
  68.8 5.0 %fusion.5 = bf16[1408,1408]{1,0:T(8,128)(2,1)} fusion(bf16[1408,1408]{1,0:T(8,128)(2,1)} %copy.38, f32[11,1408]{1,0:T(8,128)S(1)} %multiply_exponential_fusion.1), kind=kLoop, calls=%fused_computation.13 | loop fusion | flops 5947392 | bytes 7991808 | tf_op jit(solution)/shard_map/convert_element_type | solution.py:40
  73.8 85.8 %all-gather.3.cloned.1.call-done = bf16[1408,4224]{0,1:T(8,128)(2,1)} async-done(((bf16[1408,264]{0,1:T(8,128)(2,1)}), bf16[1408,4224]{0,1:T(8,128)(2,1)}) %all-gather.3.cloned.1.call-update) | async-done | bytes 11894800 | tf_op jit(solution)/shard_map/all_gather | solution.py:103
  159.6 16.0 %copy.32 = bf16[1408,4224]{1,0:T(8,128)(2,1)} copy(bf16[1408,4224]{0,1:T(8,128)(2,1)} %all-gather.3.cloned.1.call-done) | data formatting | bytes 23789568 | tf_op jit(solution)/shard_map/all_gather | solution.py:103
  175.6 6.8 %fusion.1 = bf16[1408,4224]{1,0:T(8,128)(2,1)S(1)} fusion(bf16[1408,4224]{1,0:T(8,128)(2,1)} %copy.32, f32[11,4224]{1,0:T(8,128)S(1)} %multiply_exponential_fusion), kind=kLoop, calls=%fused_computation.7 | loop fusion | flops 17842176 | bytes 23975424 | tf_op jit(solution)/shard_map/convert_element_type | solution.py:40
  182.4 9.2 %convolution_convert_fusion = bf16[514,4224]{1,0:T(8,128)(2,1)} fusion(bf16[1408,4224]{1,0:T(8,128)(2,1)S(1)} %fusion.1, bf16[514,1408]{1,0:T(8,128)(2,1)S(1)} %copy-done.1, f32[1408]{0:T(1024)S(1)} %copy-done.5, f32[514]{0:T(1024)S(1)} %add_rsqrt_fusion.1, f32[514]{0:T(1024)S(1)} %broadcast_multiply_fusion), kind=kOutput, calls=%fused_computation.14 | convolution fusion | flops 6119708672 | bytes 17694224 | tf_op jit(solution)/shard_map/dot_general | solution.py:67
  191.6 14.9 %reshape.165 = bf16[2,257,3,16,88]{4,3,2,1,0:T(8,128)(2,1)} reshape(bf16[514,4224]{1,0:T(8,128)(2,1)} %convolution_convert_fusion) | data formatting | bytes 8684544 | tf_op jit(solution)/shard_map/reshape | solution.py:52
  206.4 5.3 %fusion.34 = (bf16[2,257,1,16,88]{4,3,2,1,0:T(8,128)(2,1)}, bf16[2,257,1,16,88]{4,3,2,1,0:T(8,128)(2,1)S(1)}, bf16[2,257,1,16,88]{4,3,2,1,0:T(8,128)(2,1)S(1)}) fusion(bf16[2,257,3,16,88]{4,3,2,1,0:T(8,128)(2,1)} %reshape.165), kind=kLoop, calls=%fused_computation.104 | loop fusion | bytes 8684544 | tf_op jit(solution)/shard_map/slice | solution.py:61
  211.8 7.2 %fusion.13 = f32[2,16,257,257]{2,3,1,0:T(8,128)} fusion(bf16[2,257,1,16,88]{4,3,2,1,0:T(8,128)(2,1)S(1)} %get-tuple-element.3, bf16[2,257,1,16,88]{4,3,2,1,0:T(8,128)(2,1)S(1)} %get-tuple-element.4), kind=kOutput, calls=%fused_computation.28 | convolution fusion | flops 371987968 | bytes 11349120 | tf_op jit(solution)/shard_map/gqhd,gkhd->ghqk/dot_general | solution.py:53
  218.9 16.6 %fusion.35 = (f32[2,16,257]{2,1,0:T(8,128)S(1)}, f32[2,16,257,257]{2,3,1,0:T(8,128)}) fusion(f32[2,16,257,257]{2,3,1,0:T(8,128)} %fusion.13), kind=kOutput, calls=%fused_computation.105 | output fusion | flops 8454528 | bytes 16941440 | tf_op jit(solution)/shard_map/sub | solution.py:57
  235.6 4.4 %copy.49 = bf16[2,257,1,16,88]{1,4,3,0,2:T(8,128)(2,1)} copy(bf16[2,257,1,16,88]{4,3,2,1,0:T(8,128)(2,1)} %get-tuple-element.2) | data formatting | bytes 2894848
  240.0 8.5 %convert_bitcast_fusion = bf16[2,257,16,88]{1,3,2,0:T(8,128)(2,1)} fusion(f32[2,16,257,257]{2,3,1,0:T(8,128)} %get-tuple-element.22, f32[2,16,257]{2,1,0:T(8,128)S(1)} %get-tuple-element.21, bf16[2,257,1,16,88]{1,4,3,0,2:T(8,128)(2,1)} %copy.49), kind=kOutput, calls=%fused_computation.31 | convolution fusion | flops 376938816 | bytes 11382016 | tf_op jit(solution)/shard_map/ghqk,gkhd->gqhd/dot_general | solution.py:60
  248.5 4.5 %copy.37 = bf16[2,257,16,88]{3,2,1,0:T(8,128)(2,1)} copy(bf16[2,257,16,88]{1,3,2,0:T(8,128)(2,1)} %convert_bitcast_fusion) | data formatting | bytes 2894848 | tf_op jit(solution)/shard_map/convert_element_type | solution.py:63
  253.1 5.1 %reshape.166 = bf16[514,1408]{1,0:T(8,128)(2,1)} reshape(bf16[2,257,16,88]{3,2,1,0:T(8,128)(2,1)} %copy.37) | data formatting | bytes 2894848 | tf_op jit(solution)/shard_map/reshape | solution.py:63
  258.1 7.3 %multiply_reduce_fusion.1 = (f32[514]{0:T(1024)S(1)}, f32[514,1408]{1,0:T(8,128)}) fusion(bf16[514,1408]{1,0:T(8,128)(2,1)} %reshape.166, bf16[1408,1408]{1,0:T(8,128)(2,1)} %fusion.5, bf16[514,1408]{1,0:T(8,128)(2,1)} %param.9), kind=kOutput, calls=%fused_computation.26 | convolution fusion | flops 2040867328 | bytes 9756680 | tf_op jit(solution)/shard_map/dot_general | solution.py:67
  265.4 12.3 %scatter_custom_fusion.1 = bf16[544,1408]{1,0:T(8,128)(2,1)} fusion(s32[514]{0:T(1024)S(1)} %fusion.30, bf16[]{:T(256)} %constant.138.clone.1, f32[514,1408]{1,0:T(8,128)} %get-tuple-element.24, f32[514]{0:T(1024)S(1)} %add_rsqrt_fusion), kind=kCustom, calls=%fused_computation.36 | custom fusion | flops 1447424 | bytes 4430850 | tf_op jit(solution)/shard_map/scatter | solution.py:122
  277.7 2.6 reshape.170
  280.3 4.6 %all-to-all-start.1 = ((bf16[16,34,1408]{2,1,0:T(8,128)(2,1)}), bf16[16,34,1408]{2,1,0:T(8,128)(2,1)}, u32[]{:S(2)}, u32[]{:S(2)}) async-start(bf16[16,34,1408]{2,1,0:T(8,128)(2,1)} %reshape.170), calls=%async_computation.1 | async-start | bytes 3604480 | tf_op jit(solution)/shard_map/all_to_all | solution.py:134
  285.4 0.1 copy.46
  285.5 0.2 reshape.191
  285.8 0.3 copy.44
  286.0 34.7 %all-to-all-done.1 = bf16[16,34,1408]{2,1,0:T(8,128)(2,1)} async-done(((bf16[16,34,1408]{2,1,0:T(8,128)(2,1)}), bf16[16,34,1408]{2,1,0:T(8,128)(2,1)}, u32[]{:S(2)}, u32[]{:S(2)}) %all-to-all-start.1) | async-done | bytes 1531936 | tf_op jit(solution)/shard_map/all_to_all | solution.py:134
  320.8 2.6 reshape.215
  323.3 3.3 fusion.36
  326.7 1.4 copy.47
  328.1 22.9 %gather_fusion.2 = bf16[2176,128]{1,0:T(8,128)(2,1)S(1)} fusion(bf16[544,8,128]{2,1,0:T(8,128)(2,1)} %copy.47, s32[2176]{0:T(1024)S(1)} %reshape.191), kind=kCustom, calls=%fused_computation.2 | custom fusion | bytes 1131520 | tf_op jit(solution)/shard_map/jit(take_along_axis)/gather | solution.py:83
  351.0 0.8 select_convert_fusion
  351.8 0.3 dynamic-slice_bitcast_fusion
  352.1 1.1 collective-permute-start
  353.1 3.2 multiply_convert_fusion
  356.3 2.9 collective-permute-start.1
  359.2 5.4 %collective-permute-start.2 = (bf16[1,34,4,128]{3,2,1,0:T(4,128)(2,1)S(1)}, bf16[1,34,4,128]{3,2,1,0:T(4,128)(2,1)S(1)}, u32[]{:S(2)}, u32[]{:S(2)}) collective-permute-start(bf16[1,34,4,128]{3,2,1,0:T(4,128)(2,1)S(1)} %get-tuple-element.17), channel_id=1, source_target_pairs={{0,3},{1,4},{2,5},{3,6},{4,7},{5,8},{6,9},{7,10},{8,11},{9,12},{10... | collective-permute-start | bytes 104456 | tf_op jit(solution)/shard_map/ppermute | solution.py:30
  364.6 0.7 collective-permute-start.3
  365.2 0.1 collective-permute-start.4
  365.4 1.6 collective-permute-start.5
  367.0 3.7 collective-permute-start.6
  370.7 0.4 collective-permute-start.7
  371.1 1.8 collective-permute-start.8
  372.9 1.8 collective-permute-start.9
  374.8 2.7 collective-permute-start.10
  377.5 1.5 collective-permute-start.11
  379.1 0.4 collective-permute-start.12
  379.5 1.2 collective-permute-start.13
  380.8 3.5 collective-permute-start.14
  384.5 1.4 collective-permute-done.14
  385.9 0.8 copy-done.2
  386.7 2.1 gather_fusion
  388.8 3.1 gather_fusion.1
  (61 shorter events, 0.9 us)
Async XLA Ops:
  7.2 316.2 %copy-start = (bf16[1024,1408]{1,0:T(8,128)(2,1)S(1)}, bf16[1024,1408]{1,0:T(8,128)(2,1)}, u32[]{:S(2)}) copy-start(bf16[1024,1408]{1,0:T(8,128)(2,1)} %param.15) | copy-start | bytes 8650756
  7.2 21.8 %copy-start.3 = (s32[11,4224]{1,0:T(8,128)S(1)}, s32[11,4224]{1,0:T(8,128)}, u32[]{:S(2)}) copy-start(s32[11,4224]{1,0:T(8,128)} %param.12) | copy-start | bytes 557572
  7.2 55.4 %all-gather.5.cloned.1.call-start = ((), (), s32[]{:S(2)}) async-start(), calls=%async_computation.3 | async-start | bytes 4212736 | tf_op jit(solution)/shard_map/all_gather | solution.py:107
  7.9 151.7 %all-gather.3.cloned.1.call-start = ((), (), s32[]{:S(2)}) async-start(), calls=%async_computation.2 | async-start | bytes 12638208 | tf_op jit(solution)/shard_map/all_gather | solution.py:103
  17.1 11.9 %copy-start.4 = (s32[11,1408]{1,0:T(8,128)S(1)}, s32[11,1408]{1,0:T(8,128)}, u32[]{:S(2)}) copy-start(s32[11,1408]{1,0:T(8,128)} %param.14) | copy-start | bytes 185860
  17.9 262.4 %all-to-all-start = ((bf16[16,34,4]{1,2,0:T(4,128)(2,1)}), bf16[16,34,4]{1,2,0:T(4,128)(2,1)S(1)}, u32[]{:S(2)}, u32[]{:S(2)}) async-start(bf16[16,34,4]{1,2,0:T(4,128)(2,1)} %copy.43), calls=%async_computation | async-start | bytes 32768 | tf_op jit(solution)/shard_map/all_to_all | solution.py:135
  175.5 6.8 %copy-start.1 = (bf16[514,1408]{1,0:T(8,128)(2,1)S(1)}, bf16[514,1408]{1,0:T(8,128)(2,1)}, u32[]{:S(2)}) copy-start(bf16[514,1408]{1,0:T(8,128)(2,1)} %param.9) | copy-start | bytes 4342276
  175.6 6.8 %copy-start.5 = (f32[1408]{0:T(1024)S(1)}, f32[1408]{0:T(1024)}, u32[]{:S(2)}) copy-start(f32[1408]{0:T(1024)} %param.10) | copy-start | bytes 16900
  280.3 40.4 %all-to-all-start.1 = ((bf16[16,34,1408]{2,1,0:T(8,128)(2,1)}), bf16[16,34,1408]{2,1,0:T(8,128)(2,1)}, u32[]{:S(2)}, u32[]{:S(2)}) async-start(bf16[16,34,1408]{2,1,0:T(8,128)(2,1)} %reshape.170), calls=%async_computation.1 | async-start | bytes 3604480 | tf_op jit(solution)/shard_map/all_to_all | solution.py:134
  352.1 13.3 %collective-permute-start = (bf16[1,34,4,128]{3,2,1,0:T(4,128)(2,1)S(1)}, bf16[1,34,4,128]{3,2,1,0:T(4,128)(2,1)S(1)}, u32[]{:S(2)}, u32[]{:S(2)}) collective-permute-start(bf16[1,34,4,128]{3,2,1,0:T(4,128)(2,1)S(1)} %get-tuple-element.19), channel_id=1, source_target_pairs={{0,1},{1,2},{2,3},{3,4},{4,5},{5,6},{6,7},{7,8},{8,9},{9,10},{10,1... | collective-permute-start | bytes 104456 | tf_op jit(solution)/shard_map/ppermute | solution.py:30
  356.3 10.7 %collective-permute-start.1 = (bf16[1,34,4,128]{3,2,1,0:T(4,128)(2,1)S(1)}, bf16[1,34,4,128]{3,2,1,0:T(4,128)(2,1)S(1)}, u32[]{:S(2)}, u32[]{:S(2)}) collective-permute-start(bf16[1,34,4,128]{3,2,1,0:T(4,128)(2,1)S(1)} %get-tuple-element.18), channel_id=1, source_target_pairs={{0,2},{1,3},{2,4},{3,5},{4,6},{5,7},{6,8},{7,9},{8,10},{9,11},{10,... | collective-permute-start | bytes 104456 | tf_op jit(solution)/shard_map/ppermute | solution.py:30
  359.2 11.5 %collective-permute-start.2 = (bf16[1,34,4,128]{3,2,1,0:T(4,128)(2,1)S(1)}, bf16[1,34,4,128]{3,2,1,0:T(4,128)(2,1)S(1)}, u32[]{:S(2)}, u32[]{:S(2)}) collective-permute-start(bf16[1,34,4,128]{3,2,1,0:T(4,128)(2,1)S(1)} %get-tuple-element.17), channel_id=1, source_target_pairs={{0,3},{1,4},{2,5},{3,6},{4,7},{5,8},{6,9},{7,10},{8,11},{9,12},{10... | collective-permute-start | bytes 104456 | tf_op jit(solution)/shard_map/ppermute | solution.py:30
  364.6 6.5 %collective-permute-start.3 = (bf16[1,34,4,128]{3,2,1,0:T(4,128)(2,1)S(1)}, bf16[1,34,4,128]{3,2,1,0:T(4,128)(2,1)S(1)}, u32[]{:S(2)}, u32[]{:S(2)}) collective-permute-start(bf16[1,34,4,128]{3,2,1,0:T(4,128)(2,1)S(1)} %get-tuple-element.16), channel_id=1, source_target_pairs={{0,4},{1,5},{2,6},{3,7},{4,8},{5,9},{6,10},{7,11},{8,12},{9,13},{1... | collective-permute-start | bytes 104456 | tf_op jit(solution)/shard_map/ppermute | solution.py:30
  365.2 7.7 %collective-permute-start.4 = (bf16[1,34,4,128]{3,2,1,0:T(4,128)(2,1)S(1)}, bf16[1,34,4,128]{3,2,1,0:T(4,128)(2,1)S(1)}, u32[]{:S(2)}, u32[]{:S(2)}) collective-permute-start(bf16[1,34,4,128]{3,2,1,0:T(4,128)(2,1)S(1)} %get-tuple-element.15), channel_id=1, source_target_pairs={{0,5},{1,6},{2,7},{3,8},{4,9},{5,10},{6,11},{7,12},{8,13},{9,14},{... | collective-permute-start | bytes 104456 | tf_op jit(solution)/shard_map/ppermute | solution.py:30
  365.4 9.4 %collective-permute-start.5 = (bf16[1,34,4,128]{3,2,1,0:T(4,128)(2,1)S(1)}, bf16[1,34,4,128]{3,2,1,0:T(4,128)(2,1)S(1)}, u32[]{:S(2)}, u32[]{:S(2)}) collective-permute-start(bf16[1,34,4,128]{3,2,1,0:T(4,128)(2,1)S(1)} %get-tuple-element.14), channel_id=1, source_target_pairs={{0,6},{1,7},{2,8},{3,9},{4,10},{5,11},{6,12},{7,13},{8,14},{9,15},... | collective-permute-start | bytes 104456 | tf_op jit(solution)/shard_map/ppermute | solution.py:30
  367.0 10.5 %collective-permute-start.6 = (bf16[1,34,4,128]{3,2,1,0:T(4,128)(2,1)S(1)}, bf16[1,34,4,128]{3,2,1,0:T(4,128)(2,1)S(1)}, u32[]{:S(2)}, u32[]{:S(2)}) collective-permute-start(bf16[1,34,4,128]{3,2,1,0:T(4,128)(2,1)S(1)} %get-tuple-element.13), channel_id=1, source_target_pairs={{0,7},{1,8},{2,9},{3,10},{4,11},{5,12},{6,13},{7,14},{8,15},{9,0},... | collective-permute-start | bytes 104456 | tf_op jit(solution)/shard_map/ppermute | solution.py:30
  370.7 8.4 %collective-permute-start.7 = (bf16[1,34,4,128]{3,2,1,0:T(4,128)(2,1)S(1)}, bf16[1,34,4,128]{3,2,1,0:T(4,128)(2,1)S(1)}, u32[]{:S(2)}, u32[]{:S(2)}) collective-permute-start(bf16[1,34,4,128]{3,2,1,0:T(4,128)(2,1)S(1)} %get-tuple-element.12), channel_id=1, source_target_pairs={{0,8},{1,9},{2,10},{3,11},{4,12},{5,13},{6,14},{7,15},{8,0},{9,1},... | collective-permute-start | bytes 104456 | tf_op jit(solution)/shard_map/ppermute | solution.py:30
  371.1 8.4 %collective-permute-start.8 = (bf16[1,34,4,128]{3,2,1,0:T(4,128)(2,1)S(1)}, bf16[1,34,4,128]{3,2,1,0:T(4,128)(2,1)S(1)}, u32[]{:S(2)}, u32[]{:S(2)}) collective-permute-start(bf16[1,34,4,128]{3,2,1,0:T(4,128)(2,1)S(1)} %get-tuple-element.11), channel_id=1, source_target_pairs={{0,9},{1,10},{2,11},{3,12},{4,13},{5,14},{6,15},{7,0},{8,1},{9,2},... | collective-permute-start | bytes 104456 | tf_op jit(solution)/shard_map/ppermute | solution.py:30
  372.9 7.9 %collective-permute-start.9 = (bf16[1,34,4,128]{3,2,1,0:T(4,128)(2,1)S(1)}, bf16[1,34,4,128]{3,2,1,0:T(4,128)(2,1)S(1)}, u32[]{:S(2)}, u32[]{:S(2)}) collective-permute-start(bf16[1,34,4,128]{3,2,1,0:T(4,128)(2,1)S(1)} %get-tuple-element.10), channel_id=1, source_target_pairs={{0,10},{1,11},{2,12},{3,13},{4,14},{5,15},{6,0},{7,1},{8,2},{9,3},... | collective-permute-start | bytes 104456 | tf_op jit(solution)/shard_map/ppermute | solution.py:30
  374.8 9.5 %collective-permute-start.10 = (bf16[1,34,4,128]{3,2,1,0:T(4,128)(2,1)S(1)}, bf16[1,34,4,128]{3,2,1,0:T(4,128)(2,1)S(1)}, u32[]{:S(2)}, u32[]{:S(2)}) collective-permute-start(bf16[1,34,4,128]{3,2,1,0:T(4,128)(2,1)S(1)} %get-tuple-element.9), channel_id=1, source_target_pairs={{0,11},{1,12},{2,13},{3,14},{4,15},{5,0},{6,1},{7,2},{8,3},{9,4},{... | collective-permute-start | bytes 104456 | tf_op jit(solution)/shard_map/ppermute | solution.py:30
  377.5 6.8 %collective-permute-start.11 = (bf16[1,34,4,128]{3,2,1,0:T(4,128)(2,1)S(1)}, bf16[1,34,4,128]{3,2,1,0:T(4,128)(2,1)S(1)}, u32[]{:S(2)}, u32[]{:S(2)}) collective-permute-start(bf16[1,34,4,128]{3,2,1,0:T(4,128)(2,1)S(1)} %get-tuple-element.8), channel_id=1, source_target_pairs={{0,12},{1,13},{2,14},{3,15},{4,0},{5,1},{6,2},{7,3},{8,4},{9,5},{1... | collective-permute-start | bytes 104456 | tf_op jit(solution)/shard_map/ppermute | solution.py:30
  379.1 5.3 %collective-permute-start.12 = (bf16[1,34,4,128]{3,2,1,0:T(4,128)(2,1)S(1)}, bf16[1,34,4,128]{3,2,1,0:T(4,128)(2,1)S(1)}, u32[]{:S(2)}, u32[]{:S(2)}) collective-permute-start(bf16[1,34,4,128]{3,2,1,0:T(4,128)(2,1)S(1)} %get-tuple-element.7), channel_id=1, source_target_pairs={{0,13},{1,14},{2,15},{3,0},{4,1},{5,2},{6,3},{7,4},{8,5},{9,6},{10... | collective-permute-start | bytes 104456 | tf_op jit(solution)/shard_map/ppermute | solution.py:30
  379.5 4.9 %collective-permute-start.13 = (bf16[1,34,4,128]{3,2,1,0:T(4,128)(2,1)S(1)}, bf16[1,34,4,128]{3,2,1,0:T(4,128)(2,1)S(1)}, u32[]{:S(2)}, u32[]{:S(2)}) collective-permute-start(bf16[1,34,4,128]{3,2,1,0:T(4,128)(2,1)S(1)} %get-tuple-element.6), channel_id=1, source_target_pairs={{0,14},{1,15},{2,0},{3,1},{4,2},{5,3},{6,4},{7,5},{8,6},{9,7},{10,... | collective-permute-start | bytes 104456 | tf_op jit(solution)/shard_map/ppermute | solution.py:30
  380.8 5.1 %collective-permute-start.14 = (bf16[1,34,4,128]{3,2,1,0:T(4,128)(2,1)S(1)}, bf16[1,34,4,128]{3,2,1,0:T(4,128)(2,1)S(1)}, u32[]{:S(2)}, u32[]{:S(2)}) collective-permute-start(bf16[1,34,4,128]{3,2,1,0:T(4,128)(2,1)S(1)} %get-tuple-element.5), channel_id=1, source_target_pairs={{0,15},{1,0},{2,1},{3,2},{4,3},{5,4},{6,5},{7,6},{8,7},{9,8},{10,9... | collective-permute-start | bytes 104456 | tf_op jit(solution)/shard_map/ppermute | solution.py:30
  385.9 0.8 copy-start.2
Sparse Core Ops, SparseCore 0:
  10.2 52.3 all-gather.4
  64.7 94.8 all-gather.2
